TPU v7x, 32 devices: a whole 2x2x4 slice. The times are simulated.
32 devices in a mesh: seq: 16 (over z, x, core), fsdp: 2 (over y).
Axes of the slice: x: 2, y: 2, z: 4, core: 2. Of those that a mesh axis runs over, the one named last changes fastest.
Arguments:
- inputs: bfloat16 [2, 16384, 1024], P(None, 'seq', 'fsdp'), may hold values from -6 to 6
- first_factor: bfloat16 [128, 128, 128], P('seq'), may hold values from -0.5 to 0.5
- second_factor: bfloat16 [128, 128, 128], P('seq'), may hold values from -0.5 to 0.5
- gate_scale: float32 [1024], P('fsdp'), may hold values from -2 to 2
- gate_bias: float32 [1024], P('fsdp'), may hold values from -3 to 3
- in_weight: bfloat16 [1024, 4096], P('seq', 'fsdp'), may hold values from -0.1875 to 0.1875
- out_weight: bfloat16 [4096, 1024], P('fsdp', 'seq'), may hold values from -0.09375 to 0.09375
- cotangent: bfloat16 [2, 16384, 1024], P(None, 'seq', 'fsdp'), may hold values from -6 to 6
Outputs:
- result: bfloat16 [2, 16384, 1024], P(None, 'seq', 'fsdp')
- input_grad: bfloat16 [2, 16384, 1024], P(None, 'seq', 'fsdp')
- grad_in: float32 [1024, 4096], P('seq', 'fsdp')
- grad_out: float32 [4096, 1024], P('fsdp', 'seq')
All inputs are finite; a program needn't handle non-finite values.
Results may differ from a plain program's by a relative error of at most 0.0075.
Values may be sent and summed in bfloat16 or wider, within the bound.
A program may use at most 192 MiB of HBM per device.

v0:
```python
import jax
import jax.numpy as jnp
from jax import lax
from jax.sharding import PartitionSpec as P


def body(
    inputs, first_factor, second_factor, gate_scale, gate_bias, in_weight, out_weight, cotangent
):
    seq_count, tok_rows, chan_count = inputs.shape
    blocks = first_factor.shape[0]
    block_size = first_factor.shape[1]
    row_count = seq_count * tok_rows
    groups = lax.axis_size("fsdp")
    gate_gain = gate_scale.reshape(1, 1, 1, chan_count)
    gate_shift = gate_bias.reshape(1, 1, 1, chan_count)
    source = inputs.reshape(seq_count, blocks, block_size, chan_count)
    section_one = jnp.einsum(
        "mkn,smnc->smkc", first_factor, source, preferred_element_type=jnp.float32
    ).astype(jnp.bfloat16)
    turned, source_cols = (
        lax.all_to_all(section_one, "seq", split_axis=2, concat_axis=1, tiled=True),
        lax.all_to_all(source, "seq", split_axis=2, concat_axis=1, tiled=True),
    )
    section_two = jnp.einsum(
        "kjm,smkc->sjkc", second_factor, turned, preferred_element_type=jnp.float32
    ).astype(jnp.bfloat16)
    section_two = lax.optimization_barrier(section_two)
    gate_cols = jax.nn.sigmoid(gate_gain * source_cols.astype(jnp.float32) + gate_shift)
    gated_cols = (gate_cols * section_two.astype(jnp.float32)).astype(jnp.bfloat16)
    mixed_grid = lax.all_to_all(gated_cols, "seq", split_axis=1, concat_axis=2, tiled=True)
    mixed = mixed_grid.reshape(row_count, chan_count)
    full_in = lax.all_gather(in_weight, "seq", axis=0, tiled=True)
    full_out = lax.all_gather(out_weight, "seq", axis=1, tiled=True)
    mixed_all = lax.all_gather(mixed, "fsdp", axis=1, tiled=True)
    pre_act = jnp.dot(mixed_all, full_in, preferred_element_type=jnp.float32)
    hidden = jax.nn.silu(pre_act).astype(jnp.bfloat16)
    partial_out = jnp.dot(hidden, full_out, preferred_element_type=jnp.float32)
    received = lax.all_to_all(partial_out, "fsdp", split_axis=1, concat_axis=0, tiled=True)
    branch_sum = jnp.sum(received.reshape(groups, row_count, chan_count), axis=0)
    result = (
        (mixed.astype(jnp.float32) + branch_sum)
        .astype(jnp.bfloat16)
        .reshape(seq_count, tok_rows, chan_count)
    )
    upstream = cotangent.reshape(row_count, chan_count)
    upstream_all = lax.all_gather(upstream, "fsdp", axis=1, tiled=True)
    hidden_grad = lax.dot_general(
        upstream_all, full_out, (((1,), (1,)), ((), ())), preferred_element_type=jnp.float32
    )
    sigma = jax.nn.sigmoid(pre_act)
    pre_grad = (hidden_grad * sigma * (1.0 + pre_act * (1.0 - sigma))).astype(jnp.bfloat16)
    out_term = lax.dot_general(
        hidden, upstream_all, (((0,), (0,)), ((), ())), preferred_element_type=jnp.float32
    )
    grad_out = lax.psum_scatter(out_term, "seq", scatter_dimension=1, tiled=True) * (
        1.0 / block_size
    )
    in_term = lax.dot_general(
        mixed_all, pre_grad, (((0,), (0,)), ((), ())), preferred_element_type=jnp.float32
    )
    grad_in = lax.psum_scatter(in_term, "seq", scatter_dimension=0, tiled=True) * (1.0 / block_size)
    back_term = lax.dot_general(
        pre_grad, full_in, (((1,), (1,)), ((), ())), preferred_element_type=jnp.float32
    )
    back_pieces = lax.all_to_all(back_term, "fsdp", split_axis=1, concat_axis=0, tiled=True)
    back_sum = jnp.sum(back_pieces.reshape(groups, row_count, chan_count), axis=0)
    mixed_grad = (
        (upstream.astype(jnp.float32) + back_sum)
        .astype(jnp.bfloat16)
        .reshape(seq_count, blocks, block_size, chan_count)
    )
    grad_cols = lax.all_to_all(mixed_grad, "seq", split_axis=2, concat_axis=1, tiled=True).astype(
        jnp.float32
    )
    second_grad = (grad_cols * gate_cols).astype(jnp.bfloat16)
    gate_term = (
        grad_cols * section_two.astype(jnp.float32) * gate_cols * (1.0 - gate_cols) * gate_gain
    )
    gate_back = lax.all_to_all(
        gate_term.astype(jnp.bfloat16), "seq", split_axis=1, concat_axis=2, tiled=True
    ).astype(gate_term.dtype)
    first_grad = jnp.einsum(
        "kjm,sjkc->smkc", second_factor, second_grad, preferred_element_type=jnp.float32
    ).astype(jnp.bfloat16)
    first_rows = lax.all_to_all(first_grad, "seq", split_axis=1, concat_axis=2, tiled=True)
    input_sum = (
        jnp.einsum("mkn,smkc->smnc", first_factor, first_rows, preferred_element_type=jnp.float32)
        + gate_back
    )
    input_grad = input_sum.astype(jnp.bfloat16).reshape(seq_count, tok_rows, chan_count)
    return (result, input_grad, grad_in, grad_out)


def solution(mesh):
    in_specs = (
        P(None, "seq", "fsdp"),
        P("seq", None, None),
        P("seq", None, None),
        P("fsdp"),
        P("fsdp"),
        P("seq", "fsdp"),
        P("fsdp", "seq"),
        P(None, "seq", "fsdp"),
    )
    out_specs = (P(None, "seq", "fsdp"), P(None, "seq", "fsdp"), P("seq", "fsdp"), P("fsdp", "seq"))
    return jax.shard_map(body, mesh=mesh, in_specs=in_specs, out_specs=out_specs, check_vma=False)
```

profile of v0, /device:TPU:11, one launch (start us, length us, event | category | flops | bytes accessed | tf_op | source)
XLA Modules:
  0.0 827.8 jit_solution(12045572904759130662)
XLA Ops:
  7.2 4.2 copy.79
  11.4 6.6 all-to-all-start
  17.9 3.7 convert_bitcast_fusion.5
  21.6 6.2 copy.84
  27.8 37.5 %all-to-all-done = bf16[2,8,128,512]{3,1,0,2:T(8,128)(2,1)S(1)} async-done(((bf16[2,8,128,512]{3,1,0,2:T(8,128)(2,1)}), bf16[2,8,128,512]{3,1,0,2:T(8,128)(2,1)S(1)}, u32[]{:S(2)}, u32[]{:S(2)}) %all-to-all-start) | async-done | bytes 2097184 | tf_op jit(solution)/shard_map/all_to_all | solution.py:23
  65.3 4.9 all-to-all-start.1
  72.2 2.6 copy.81
  74.9 5.3 copy.82
  80.2 61.0 %all-to-all-done.1 = bf16[2,8,128,512]{3,0,1,2:T(2,128)(2,1)} async-done(((bf16[2,8,128,512]{3,0,1,2:T(2,128)(2,1)}), bf16[2,8,128,512]{3,0,1,2:T(2,128)(2,1)}, u32[]{:S(2)}, u32[]{:S(2)}) %all-to-all-start.1) | async-done | bytes 2097184 | tf_op jit(solution)/shard_map/all_to_all | solution.py:22
  141.2 2.8 copy.132
  146.8 2.7 fusion
  149.6 5.0 copy.88
  154.6 52.1 %all_to_all.104 = bf16[2,128,8,512]{3,0,2,1:T(2,128)(2,1)S(1)} all-to-all(bf16[2,128,8,512]{3,0,2,1:T(2,128)(2,1)S(1)} %copy.88), channel_id=1, replica_groups=mesh['seq'=16,'fsdp'=2] {'seq'}, dimensions={1} | all-to-all | bytes 4194304 | tf_op jit(solution)/shard_map/all_to_all | solution.py:31
  211.5 54.9 %all-gather.5.cloned.1.call-done = bf16[2048,1024]{1,0:T(8,128)(2,1)} async-done(((bf16[2048,512]{1,0:T(8,128)(2,1)}), bf16[2048,1024]{1,0:T(8,128)(2,1)}) %all-gather.5.cloned.1.call-update) | async-done | bytes 4194320 | tf_op jit(solution)/shard_map/all_gather | solution.py:35
  266.4 18.6 %multiply_convert_fusion.1 = (bf16[2048,2048]{1,0:T(8,128)(2,1)}, f32[2048,2048]{1,0:T(8,128)}) fusion(bf16[2048,1024]{1,0:T(8,128)(2,1)} %all-gather.5.cloned.1.call-done, bf16[1024,2048]{1,0:T(8,128)(2,1)} %all-gather.7.cloned.1.call-done), kind=kOutput, calls=%fused_computation.1 | convolution fusion | flops 8610906112 | bytes 33554432 | tf_op jit(solution)/shard_map/dot_general | solution.py:36
  285.0 39.7 %all-gather.11.cloned.1.call-done = bf16[2048,1024]{1,0:T(8,128)(2,1)} async-done(((bf16[2048,512]{1,0:T(8,128)(2,1)}), bf16[2048,1024]{1,0:T(8,128)(2,1)}) %all-gather.11.cloned.1.call-update) | async-done | bytes 4194320 | tf_op jit(solution)/shard_map/all_gather | solution.py:47
  324.7 52.1 %all-gather.9.cloned.1.call-done = bf16[2048,1024]{0,1:T(8,128)(2,1)} async-done(((bf16[2048,64]{0,1:T(8,128)(2,1)}), bf16[2048,1024]{0,1:T(8,128)(2,1)}) %all-gather.9.cloned.1.call-update) | async-done | bytes 4194320 | tf_op jit(solution)/shard_map/all_gather | solution.py:34
  376.9 19.2 %multiply_convert_fusion = bf16[2048,2048]{1,0:T(8,128)(2,1)S(1)} fusion(f32[2048,2048]{1,0:T(8,128)} %get-tuple-element.5, bf16[2048,1024]{1,0:T(8,128)(2,1)} %all-gather.11.cloned.1.call-done, bf16[2048,1024]{0,1:T(8,128)(2,1)} %all-gather.9.cloned.1.call-done), kind=kOutput, calls=%fused_computation | convolution fusion | flops 8627683328 | bytes 33554432 | tf_op jit(solution)/shard_map/dot_general | solution.py:48
  396.1 3.2 copy-done.14
  399.3 11.4 %fusion.25 = f32[1024,2048]{1,0:T(8,128)} fusion(bf16[2048,1024]{1,0:T(8,128)(2,1)S(1)} %copy-done.13, bf16[2048,2048]{1,0:T(8,128)(2,1)S(1)} %multiply_convert_fusion), kind=kOutput, calls=%fused_computation.40 | convolution fusion | flops 8589934592 | bytes 20971520 | tf_op jit(solution)/shard_map/dot_general | solution.py:59
  410.8 12.6 %fusion.24 = f32[2048,1024]{0,1:T(8,128)S(1)} fusion(bf16[2048,2048]{1,0:T(8,128)(2,1)} %copy-done.14, bf16[1024,2048]{1,0:T(8,128)(2,1)} %all-gather.7.cloned.1.call-done), kind=kOutput, calls=%fused_computation.39 | convolution fusion | flops 8589934592 | bytes 20971520 | tf_op jit(solution)/shard_map/dot_general | solution.py:63
  423.3 96.6 %all_to_all.105 = f32[2048,2,512]{0,2,1:T(8,128)} all-to-all(f32[2048,2,512]{0,2,1:T(8,128)S(1)} %bitcast.96), channel_id=1, replica_groups=mesh['seq'=16,'fsdp'=2] {'fsdp'}, dimensions={1} | all-to-all | bytes 16777216 | tf_op jit(solution)/shard_map/all_to_all | solution.py:66
  519.9 6.6 reduce_sum.24
  526.5 5.5 copy.113
  532.0 2.9 fusion.5
  535.0 2.5 copy.94
  537.5 6.2 all-to-all-start.5
  543.6 14.7 %fusion.23 = f32[2048,1024]{0,1:T(8,128)} fusion(bf16[2048,2048]{1,0:T(8,128)(2,1)} %get-tuple-element.4, bf16[2048,1024]{0,1:T(8,128)(2,1)} %all-gather.9.cloned.1.call-done), kind=kOutput, calls=%fused_computation.38 | convolution fusion | flops 8589934592 | bytes 20971520 | tf_op jit(solution)/shard_map/dot_general | solution.py:38
  558.3 32.7 %all-to-all-done.5 = bf16[2,8,128,512]{3,1,0,2:T(8,128)(2,1)S(1)} async-done(((bf16[2,8,128,512]{3,1,0,2:T(8,128)(2,1)}), bf16[2,8,128,512]{3,1,0,2:T(8,128)(2,1)S(1)}, u32[]{:S(2)}, u32[]{:S(2)}) %all-to-all-start.5) | async-done | bytes 2097184 | tf_op jit(solution)/shard_map/all_to_all | solution.py:73
  591.0 7.0 all-to-all-start.3
  598.0 14.7 %fusion.26 = f32[2048,1024]{0,1:T(8,128)} fusion(bf16[2048,2048]{1,0:T(8,128)(2,1)} %get-tuple-element.4, bf16[2048,1024]{1,0:T(8,128)(2,1)} %all-gather.11.cloned.1.call-done), kind=kOutput, calls=%fused_computation.41 | convolution fusion | flops 8589934592 | bytes 20971520 | tf_op jit(solution)/shard_map/dot_general | solution.py:53
  613.9 2.6 copy.96
  616.5 5.5 copy.97
  622.0 6.3 fusion.4
  628.3 6.4 copy.103
  634.7 55.5 %all-to-all-done.3 = f32[2048,2,512]{0,2,1:T(8,128)} async-done(((f32[2048,2,512]{0,2,1:T(8,128)}), f32[2048,2,512]{0,2,1:T(8,128)}, u32[]{:S(2)}, u32[]{:S(2)}) %all-to-all-start.3) | async-done | bytes 8388640 | tf_op jit(solution)/shard_map/all_to_all | solution.py:39
  690.2 5.9 all-to-all-start.7
  696.1 6.5 convert_bitcast_fusion.3
  702.6 6.4 copy.98
  708.9 51.4 %all-to-all-done.7 = bf16[2,128,8,512]{3,0,2,1:T(2,128)(2,1)} async-done(((bf16[2,128,8,512]{3,0,2,1:T(2,128)(2,1)}), bf16[2,128,8,512]{3,0,2,1:T(2,128)(2,1)}, u32[]{:S(2)}, u32[]{:S(2)}) %all-to-all-start.7) | async-done | bytes 2097184 | tf_op jit(solution)/shard_map/all_to_all | solution.py:80
  760.3 5.0 all-to-all-start.6
  765.3 2.6 copy.90
  767.9 6.6 reduce_sum.22
  774.5 5.3 copy.112
  779.8 5.5 fusion.7
  785.3 2.0 copy.104
  787.3 25.5 %all-to-all-done.6 = bf16[2,128,8,512]{3,0,2,1:T(2,128)(2,1)} async-done(((bf16[2,128,8,512]{3,0,2,1:T(2,128)(2,1)}), bf16[2,128,8,512]{3,0,2,1:T(2,128)(2,1)}, u32[]{:S(2)}, u32[]{:S(2)}) %all-to-all-start.6) | async-done | bytes 2097184 | tf_op jit(solution)/shard_map/all_to_all | solution.py:86
  812.8 1.9 copy.99
  (54 shorter events, 16.9 us)
Async XLA Ops:
  7.2 137.1 %copy-start = (bf16[8,128,128]{2,1,0:T(8,128)(2,1)S(1)}, bf16[8,128,128]{2,1,0:T(8,128)(2,1)}, u32[]{:S(2)}) copy-start(bf16[8,128,128]{2,1,0:T(8,128)(2,1)} %param.10) | copy-start | bytes 786436
  7.2 10.7 %copy-start.7 = (bf16[8,128,128]{2,1,0:T(8,128)(2,1)S(1)}, bf16[8,128,128]{2,1,0:T(8,128)(2,1)}, u32[]{:S(2)}) copy-start(bf16[8,128,128]{2,1,0:T(8,128)(2,1)} %param.9) | copy-start | bytes 786436
  11.4 54.0 %all-to-all-start = ((bf16[2,8,128,512]{3,1,0,2:T(8,128)(2,1)}), bf16[2,8,128,512]{3,1,0,2:T(8,128)(2,1)S(1)}, u32[]{:S(2)}, u32[]{:S(2)}) async-start(bf16[2,8,128,512]{3,1,0,2:T(8,128)(2,1)} %copy.79), calls=%async_computation | async-start | bytes 4194304 | tf_op jit(solution)/shard_map/all_to_all | solution.py:23
  65.3 75.9 %all-to-all-start.1 = ((bf16[2,8,128,512]{3,0,1,2:T(2,128)(2,1)}), bf16[2,8,128,512]{3,0,1,2:T(2,128)(2,1)}, u32[]{:S(2)}, u32[]{:S(2)}) async-start(bf16[2,8,128,512]{3,0,1,2:T(2,128)(2,1)} %copy.84), calls=%async_computation.1 | async-start | bytes 4194304 | tf_op jit(solution)/shard_map/all_to_all | solution.py:22
  70.2 141.2 %all-gather.7.cloned.1.call-start = ((), (), s32[]{:S(2)}) async-start(), calls=%async_computation.11 | async-start | bytes 4456448 | tf_op jit(solution)/shard_map/all_gather | solution.py:33
  71.0 195.4 %all-gather.5.cloned.1.call-start = ((), (), s32[]{:S(2)}) async-start(), calls=%async_computation.10 | async-start | bytes 6291456 | tf_op jit(solution)/shard_map/all_gather | solution.py:35
  143.9 2.9 copy-start.1
  144.0 2.9 copy-start.9
  144.0 2.9 copy-start.11
  145.5 1.3 copy-start.4
  207.0 1.3 copy-start.2
  209.9 114.8 %all-gather.11.cloned.1.call-start = ((), (), s32[]{:S(2)}) async-start(), calls=%async_computation.13 | async-start | bytes 6291456 | tf_op jit(solution)/shard_map/all_gather | solution.py:47
  210.6 166.2 %all-gather.9.cloned.1.call-start = ((), (), s32[]{:S(2)}) async-start(), calls=%async_computation.12 | async-start | bytes 4456448 | tf_op jit(solution)/shard_map/all_gather | solution.py:34
  211.2 605.8 %reduce-scatter.3.cloned.1.call-start = ((), (), s32[]{:S(2)}) async-start(), calls=%async_computation.14 | async-start | bytes 8912896 | tf_op jit(solution)/shard_map/reduce_scatter | solution.py:62
  376.9 22.4 %copy-start.13 = (bf16[2048,1024]{1,0:T(8,128)(2,1)S(1)}, bf16[2048,1024]{1,0:T(8,128)(2,1)}, u32[]{:S(2)}) copy-start(bf16[2048,1024]{1,0:T(8,128)(2,1)} %all-gather.5.cloned.1.call-done) | copy-start | bytes 12582916
  396.1 3.3 copy-start.14
  526.5 5.5 copy-start.6
  537.5 53.5 %all-to-all-start.5 = ((bf16[2,8,128,512]{3,1,0,2:T(8,128)(2,1)}), bf16[2,8,128,512]{3,1,0,2:T(8,128)(2,1)S(1)}, u32[]{:S(2)}, u32[]{:S(2)}) async-start(bf16[2,8,128,512]{3,1,0,2:T(8,128)(2,1)} %copy.94), calls=%async_computation.5 | async-start | bytes 4194304 | tf_op jit(solution)/shard_map/all_to_all | solution.py:73
  591.0 99.2 %all-to-all-start.3 = ((f32[2048,2,512]{0,2,1:T(8,128)}), f32[2048,2,512]{0,2,1:T(8,128)}, u32[]{:S(2)}, u32[]{:S(2)}) async-start(f32[2048,2,512]{0,2,1:T(8,128)} %bitcast.95), calls=%async_computation.3 | async-start | bytes 16777216 | tf_op jit(solution)/shard_map/all_to_all | solution.py:39
  597.9 221.0 %reduce-scatter.5.cloned.1.call-start = ((), (), s32[]{:S(2)}) async-start(), calls=%async_computation.15 | async-start | bytes 8912896 | tf_op jit(solution)/shard_map/reduce_scatter | solution.py:56
  616.5 5.5 copy-start.5
  616.5 5.5 copy-start.10
  616.5 5.5 copy-start.12
  690.2 70.1 %all-to-all-start.7 = ((bf16[2,128,8,512]{3,0,2,1:T(2,128)(2,1)}), bf16[2,128,8,512]{3,0,2,1:T(2,128)(2,1)}, u32[]{:S(2)}, u32[]{:S(2)}) async-start(bf16[2,128,8,512]{3,0,2,1:T(2,128)(2,1)} %copy.103), calls=%async_computation.7 | async-start | bytes 4194304 | tf_op jit(solution)/shard_map/all_to_all | solution.py:80
  702.6 62.7 %copy-start.3 = (bf16[2,128,8,512]{3,2,1,0:T(8,128)(2,1)S(1)}, bf16[2,128,8,512]{3,2,1,0:T(8,128)(2,1)}, u32[]{:S(2)}) copy-start(bf16[2,128,8,512]{3,2,1,0:T(8,128)(2,1)} %copy-done.2) | copy-start | bytes 6291460
  760.3 52.5 %all-to-all-start.6 = ((bf16[2,128,8,512]{3,0,2,1:T(2,128)(2,1)}), bf16[2,128,8,512]{3,0,2,1:T(2,128)(2,1)}, u32[]{:S(2)}, u32[]{:S(2)}) async-start(bf16[2,128,8,512]{3,0,2,1:T(2,128)(2,1)} %copy.98), calls=%async_computation.6 | async-start | bytes 4194304 | tf_op jit(solution)/shard_map/all_to_all | solution.py:86
  785.3 29.4 %copy-start.8 = (bf16[8,128,128]{2,1,0:T(8,128)(2,1)S(1)}, bf16[8,128,128]{2,1,0:T(8,128)(2,1)}, u32[]{:S(2)}) copy-start(bf16[8,128,128]{2,1,0:T(8,128)(2,1)} %param.9) | copy-start | bytes 786436
Sparse Core Ops, SparseCore 0:
  73.2 71.5 all-gather.6
  210.0 56.3 all-gather.4
  267.9 56.7 all-gather.10
  326.7 50.0 all-gather.8
  410.9 103.7 reduce-scatter.2
  612.8 132.9 reduce-scatter.4
where the time goes:
time: 837 us; the launch traced here: 828 us
  waiting for transfers between devices  412 us (49%)
  blocking collectives  149 us (18%)
  matrix products  103 us (12%)
  local copies, waits for them, and re-layouts  76.3 us (9%)
  other arithmetic  36.9 us (4%)
  starting transfers between devices  35.8 us (4%)
  between operations  14.5 us (2%)
    all_to_all x1, blocking collectives, body(): lax.all_to_all(back_term, 'fsdp', split_axis=1, concat_axis=0, tiled=True)  96.6 us
    all_to_all x1, waiting for transfers between devices, body(): lax.all_to_all(section_one, 'seq', split_axis=2, concat_axis=1, tiled=True)  61 us
    all_to_all x1, waiting for transfers between devices, body(): lax.all_to_all(partial_out, 'fsdp', split_axis=1, concat_axis=0, tiled=True)  55.5 us
    all_gather x1, waiting for transfers between devices, body(): mixed_all = lax.all_gather(mixed, 'fsdp', axis=1, tiled=True)  54.9 us
    all_gather x1, waiting for transfers between devices, body(): full_out = lax.all_gather(out_weight, 'seq', axis=1, tiled=True)  52.1 us
    all_to_all x1, blocking collectives, body(): lax.all_to_all(gated_cols, 'seq', split_axis=1, concat_axis=2, tiled=True)  52.1 us
    all_to_all x1, waiting for transfers between devices, body(): lax.all_to_all(gate_term.astype(jnp.bfloat16), 'seq', split_axis=1, conca...  51.4 us
    all_gather x1, waiting for transfers between devices, body(): upstream_all = lax.all_gather(upstream, 'fsdp', axis=1, tiled=True)  39.7 us
  transfers between devices with their start and end apart: 12, of which 9 were waited for; matrix products, arithmetic and copies ran while one was open for 21% of the time, Pallas kernels for 0%

commit v1 on v0

--- a/solution.py
+++ b/solution.py
@@ -31,7 +31,15 @@
     mixed_grid = lax.all_to_all(gated_cols, "seq", split_axis=1, concat_axis=2, tiled=True)
     mixed = mixed_grid.reshape(row_count, chan_count)
     full_in = lax.all_gather(in_weight, "seq", axis=0, tiled=True)
-    full_out = lax.all_gather(out_weight, "seq", axis=1, tiled=True)
+    ways, here = (lax.axis_size("seq"), lax.axis_index("seq"))
+    grown, reach = (out_weight, 1)
+    while reach < ways:
+        theirs = lax.ppermute(grown, "seq", [(d, d ^ reach) for d in range(ways)])
+        mine_first = jnp.concatenate([grown, theirs], axis=1)
+        theirs_first = jnp.concatenate([theirs, grown], axis=1)
+        grown = jnp.where(here & reach == 0, mine_first, theirs_first)
+        reach = 2 * reach
+    full_out = grown
     mixed_all = lax.all_gather(mixed, "fsdp", axis=1, tiled=True)
     pre_act = jnp.dot(mixed_all, full_in, preferred_element_type=jnp.float32)
     hidden = jax.nn.silu(pre_act).astype(jnp.bfloat16)

time: 837 us -> 808 us (0.965)
  waiting for transfers between devices: 412 us -> 371 us
    ppermute x0 -> x4, waiting for transfers between devices: none -> 95.6 us  [body(): theirs = lax.ppermute(grown, 'seq', [(d, d ^ reach) for d in range(ways)])]
    all_gather x1 -> x0, waiting for transfers between devices: 52.1 us -> none  [body(): full_out = lax.all_gather(out_weight, 'seq', axis=1, tiled=True)]
    all_gather x1, waiting for transfers between devices: 54.9 us -> 13.2 us  [body(): mixed_all = lax.all_gather(mixed, 'fsdp', axis=1, tiled=True)]
    all_gather x1, waiting for transfers between devices: 39.7 us -> 0.01 us  [body(): upstream_all = lax.all_gather(upstream, 'fsdp', axis=1, tiled=True)]
  transfers between devices with their start and end apart: 12 -> 15, of which waited for: 9 -> 11; matrix products, arithmetic and copies ran while one was open for 21% -> 22% of each run, Pallas kernels for 0% -> 0%
where the time goes in v1:
time: 808 us; the launch traced here: 798 us
  waiting for transfers between devices  371 us (46%)
  blocking collectives  148 us (18%)
  matrix products  111 us (14%)
  local copies, waits for them, and re-layouts  73 us (9%)
  starting transfers between devices  41.1 us (5%)
  other arithmetic  39.7 us (5%)
  between operations  14.3 us (2%)
    all_to_all x1, blocking collectives, body(): lax.all_to_all(back_term, 'fsdp', split_axis=1, concat_axis=0, tiled=True)  96.1 us
    ppermute x4, waiting for transfers between devices, body(): theirs = lax.ppermute(grown, 'seq', [(d, d ^ reach) for d in range(ways)])  95.6 us
    all_to_all x1, waiting for transfers between devices, body(): lax.all_to_all(section_one, 'seq', split_axis=2, concat_axis=1, tiled=True)  61 us
    all_to_all x1, waiting for transfers between devices, body(): lax.all_to_all(partial_out, 'fsdp', split_axis=1, concat_axis=0, tiled=True)  55.6 us
    all_to_all x1, blocking collectives, body(): lax.all_to_all(gated_cols, 'seq', split_axis=1, concat_axis=2, tiled=True)  52 us
    all_to_all x1, waiting for transfers between devices, body(): lax.all_to_all(gate_term.astype(jnp.bfloat16), 'seq', split_axis=1, conca...  51.4 us
    all_to_all x1, waiting for transfers between devices, body(): lax.all_to_all(source, 'seq', split_axis=2, concat_axis=1, tiled=True)  37.5 us
    all_to_all x1, waiting for transfers between devices, body(): lax.all_to_all(mixed_grad, 'seq', split_axis=2, concat_axis=1, tiled=True)  30.3 us
  transfers between devices with their start and end apart: 15, of which 11 were waited for; matrix products, arithmetic and copies ran while one was open for 22% of the time, Pallas kernels for 0%

profile of v1, /device:TPU:11, one launch (start us, length us, event | category | flops | bytes accessed | tf_op | source)
XLA Modules:
  0.0 798.2 jit_solution(16469230142204980038)
XLA Ops:
  7.2 4.2 copy.83
  11.3 6.6 all-to-all-start
  17.9 3.7 convert_bitcast_fusion.5
  21.6 6.2 copy.88
  27.8 37.5 %all-to-all-done = bf16[2,8,128,512]{3,1,0,2:T(8,128)(2,1)S(1)} async-done(((bf16[2,8,128,512]{3,1,0,2:T(8,128)(2,1)}), bf16[2,8,128,512]{3,1,0,2:T(8,128)(2,1)S(1)}, u32[]{:S(2)}, u32[]{:S(2)}) %all-to-all-start) | async-done | bytes 2097184 | tf_op jit(solution)/shard_map/all_to_all | solution.py:23
  65.3 4.9 all-to-all-start.1
  72.2 2.6 copy.85
  74.9 5.3 copy.86
  80.2 61.0 %all-to-all-done.1 = bf16[2,8,128,512]{3,0,1,2:T(2,128)(2,1)} async-done(((bf16[2,8,128,512]{3,0,1,2:T(2,128)(2,1)}), bf16[2,8,128,512]{3,0,1,2:T(2,128)(2,1)}, u32[]{:S(2)}, u32[]{:S(2)}) %all-to-all-start.1) | async-done | bytes 2097184 | tf_op jit(solution)/shard_map/all_to_all | solution.py:22
  141.2 2.8 copy.138
  146.9 2.7 fusion.2
  149.6 5.0 copy.92
  154.7 52.0 %all_to_all.104 = bf16[2,128,8,512]{3,0,2,1:T(2,128)(2,1)S(1)} all-to-all(bf16[2,128,8,512]{3,0,2,1:T(2,128)(2,1)S(1)} %copy.92), channel_id=1, replica_groups=mesh['seq'=16,'fsdp'=2] {'seq'}, dimensions={1} | all-to-all | bytes 4194304 | tf_op jit(solution)/shard_map/all_to_all | solution.py:31
  212.6 12.6 %collective-permute-done.1 = bf16[2048,128]{0,1:T(8,128)(2,1)S(1)} collective-permute-done((bf16[2048,128]{0,1:T(8,128)(2,1)S(1)}, bf16[2048,128]{0,1:T(8,128)(2,1)S(1)}, u32[]{:S(2)}, u32[]{:S(2)}) %collective-permute-start.1) | collective-permute-done | bytes 524320 | tf_op jit(solution)/shard_map/ppermute | solution.py:37
  225.9 23.5 %collective-permute-done.2 = bf16[2048,256]{0,1:T(8,128)(2,1)} collective-permute-done((bf16[2048,256]{0,1:T(8,128)(2,1)S(1)}, bf16[2048,256]{0,1:T(8,128)(2,1)}, u32[]{:S(2)}, u32[]{:S(2)}) %collective-permute-start.2) | collective-permute-done | bytes 1048608 | tf_op jit(solution)/shard_map/ppermute | solution.py:37
  249.4 2.5 maximum_select_fusion.1
  253.3 13.2 %all-gather.4.cloned.1.call-done = bf16[2048,1024]{1,0:T(8,128)(2,1)} async-done(((bf16[2048,512]{1,0:T(8,128)(2,1)}), bf16[2048,1024]{1,0:T(8,128)(2,1)}) %all-gather.4.cloned.1.call-update) | async-done | bytes 4194320 | tf_op jit(solution)/shard_map/all_gather | solution.py:43
  266.4 18.8 %multiply_convert_fusion = (bf16[2048,2048]{1,0:T(8,128)(2,1)}, f32[2048,2048]{1,0:T(8,128)}) fusion(bf16[2048,1024]{1,0:T(8,128)(2,1)} %all-gather.4.cloned.1.call-done, bf16[1024,2048]{1,0:T(8,128)(2,1)} %all-gather.6.cloned.1.call-done), kind=kOutput, calls=%fused_computation.3 | convolution fusion | flops 8610906112 | bytes 33554432 | tf_op jit(solution)/shard_map/dot_general | solution.py:44
  285.2 58.2 %collective-permute-done.3 = bf16[2048,512]{0,1:T(8,128)(2,1)} collective-permute-done((bf16[2048,512]{0,1:T(8,128)(2,1)S(1)}, bf16[2048,512]{0,1:T(8,128)(2,1)}, u32[]{:S(2)}, u32[]{:S(2)}) %collective-permute-start.3) | collective-permute-done | bytes 2097184 | tf_op jit(solution)/shard_map/ppermute | solution.py:37
  343.4 21.0 %fusion.1 = bf16[2048,2048]{1,0:T(8,128)(2,1)} fusion(f32[2048,2048]{1,0:T(8,128)} %get-tuple-element.5, bf16[2048,1024]{1,0:T(8,128)(2,1)} %all-gather.8.cloned.1.call-done, bf16[2048,512]{0,1:T(8,128)(2,1)} %collective-permute-done.3, bf16[2048,512]{0,1:T(8,128)(2,1)S(1)} %maximum_select_fusion.1, pred[]{:T(512)S(6)} %eq.12), kind=kOutput, calls=%fused_computation.2 | convolution fusion | flops 8646557696 | bytes 33554432 | tf_op jit(solution)/shard_map/dot_general | solution.py:56
  364.4 15.0 %fusion.29 = f32[1024,2048]{1,0:T(8,128)} fusion(bf16[2048,1024]{1,0:T(8,128)(2,1)} %all-gather.4.cloned.1.call-done, bf16[2048,2048]{1,0:T(8,128)(2,1)} %fusion.1), kind=kOutput, calls=%fused_computation.48 | convolution fusion | flops 8589934592 | bytes 20971520 | tf_op jit(solution)/shard_map/dot_general | solution.py:67
  379.4 12.6 %fusion.28 = f32[2048,1024]{0,1:T(8,128)S(1)} fusion(bf16[2048,2048]{1,0:T(8,128)(2,1)} %fusion.1, bf16[1024,2048]{1,0:T(8,128)(2,1)} %all-gather.6.cloned.1.call-done), kind=kOutput, calls=%fused_computation.47 | convolution fusion | flops 8589934592 | bytes 20971520 | tf_op jit(solution)/shard_map/dot_general | solution.py:71
  392.0 96.1 %all_to_all.105 = f32[2048,2,512]{0,2,1:T(8,128)} all-to-all(f32[2048,2,512]{0,2,1:T(8,128)S(1)} %bitcast.100), channel_id=1, replica_groups=mesh['seq'=16,'fsdp'=2] {'fsdp'}, dimensions={1} | all-to-all | bytes 16777216 | tf_op jit(solution)/shard_map/all_to_all | solution.py:74
  488.2 6.6 reduce_sum.24
  494.8 5.5 copy.119
  500.3 2.9 fusion.7
  503.2 2.5 copy.99
  505.7 8.5 %all-to-all-start.5 = ((bf16[2,8,128,512]{3,1,0,2:T(8,128)(2,1)}), bf16[2,8,128,512]{3,1,0,2:T(8,128)(2,1)S(1)}, u32[]{:S(2)}, u32[]{:S(2)}) async-start(bf16[2,8,128,512]{3,1,0,2:T(8,128)(2,1)} %copy.99), calls=%async_computation.5 | async-start | bytes 4194304 | tf_op jit(solution)/shard_map/all_to_all | solution.py:81
  514.3 17.0 %fusion.21 = f32[2048,1024]{0,1:T(8,128)} fusion(bf16[2048,2048]{1,0:T(8,128)(2,1)} %get-tuple-element.4, bf16[2048,512]{0,1:T(8,128)(2,1)} %collective-permute-done.3, bf16[2048,512]{0,1:T(8,128)(2,1)} %copy-done.7, pred[]{:T(512)S(6)} %eq.12), kind=kOutput, calls=%fused_computation.37 | convolution fusion | flops 8608808960 | bytes 20971520 | tf_op jit(solution)/shard_map/dot_general | solution.py:46
  531.3 30.3 %all-to-all-done.5 = bf16[2,8,128,512]{3,1,0,2:T(8,128)(2,1)S(1)} async-done(((bf16[2,8,128,512]{3,1,0,2:T(8,128)(2,1)}), bf16[2,8,128,512]{3,1,0,2:T(8,128)(2,1)S(1)}, u32[]{:S(2)}, u32[]{:S(2)}) %all-to-all-start.5) | async-done | bytes 2097184 | tf_op jit(solution)/shard_map/all_to_all | solution.py:81
  561.6 7.0 all-to-all-start.3
  568.6 14.6 %fusion.30 = f32[2048,1024]{0,1:T(8,128)} fusion(bf16[2048,2048]{1,0:T(8,128)(2,1)} %get-tuple-element.4, bf16[2048,1024]{1,0:T(8,128)(2,1)} %all-gather.8.cloned.1.call-done), kind=kOutput, calls=%fused_computation.49 | convolution fusion | flops 8589934592 | bytes 20971520 | tf_op jit(solution)/shard_map/dot_general | solution.py:61
  584.4 2.7 copy.101
  587.1 5.5 copy.102
  592.6 6.3 fusion.6
  598.9 6.3 copy.108
  605.2 55.6 %all-to-all-done.3 = f32[2048,2,512]{0,2,1:T(8,128)} async-done(((f32[2048,2,512]{0,2,1:T(8,128)}), f32[2048,2,512]{0,2,1:T(8,128)}, u32[]{:S(2)}, u32[]{:S(2)}) %all-to-all-start.3) | async-done | bytes 8388640 | tf_op jit(solution)/shard_map/all_to_all | solution.py:47
  660.8 5.7 all-to-all-start.7
  666.6 6.5 convert_bitcast_fusion.3
  673.1 6.4 copy.103
  679.5 51.4 %all-to-all-done.7 = bf16[2,128,8,512]{3,0,2,1:T(2,128)(2,1)} async-done(((bf16[2,128,8,512]{3,0,2,1:T(2,128)(2,1)}), bf16[2,128,8,512]{3,0,2,1:T(2,128)(2,1)}, u32[]{:S(2)}, u32[]{:S(2)}) %all-to-all-start.7) | async-done | bytes 2097184 | tf_op jit(solution)/shard_map/all_to_all | solution.py:88
  730.8 5.3 all-to-all-start.6
  736.1 2.6 copy.94
  738.7 6.6 reduce_sum.22
  745.3 5.4 copy.118
  750.7 5.5 fusion.9
  756.2 2.0 copy.109
  758.2 25.3 %all-to-all-done.6 = bf16[2,128,8,512]{3,0,2,1:T(2,128)(2,1)} async-done(((bf16[2,128,8,512]{3,0,2,1:T(2,128)(2,1)}), bf16[2,128,8,512]{3,0,2,1:T(2,128)(2,1)}, u32[]{:S(2)}, u32[]{:S(2)}) %all-to-all-start.6) | async-done | bytes 2097184 | tf_op jit(solution)/shard_map/all_to_all | solution.py:94
  (62 shorter events, 22.1 us)
Async XLA Ops:
  7.2 137.0 %copy-start = (bf16[8,128,128]{2,1,0:T(8,128)(2,1)S(1)}, bf16[8,128,128]{2,1,0:T(8,128)(2,1)}, u32[]{:S(2)}) copy-start(bf16[8,128,128]{2,1,0:T(8,128)(2,1)} %param.10) | copy-start | bytes 786436
  7.2 10.7 %copy-start.8 = (bf16[8,128,128]{2,1,0:T(8,128)(2,1)S(1)}, bf16[8,128,128]{2,1,0:T(8,128)(2,1)}, u32[]{:S(2)}) copy-start(bf16[8,128,128]{2,1,0:T(8,128)(2,1)} %param.9) | copy-start | bytes 786436
  11.3 54.0 %all-to-all-start = ((bf16[2,8,128,512]{3,1,0,2:T(8,128)(2,1)}), bf16[2,8,128,512]{3,1,0,2:T(8,128)(2,1)S(1)}, u32[]{:S(2)}, u32[]{:S(2)}) async-start(bf16[2,8,128,512]{3,1,0,2:T(8,128)(2,1)} %copy.83), calls=%async_computation | async-start | bytes 4194304 | tf_op jit(solution)/shard_map/all_to_all | solution.py:23
  65.3 75.9 %all-to-all-start.1 = ((bf16[2,8,128,512]{3,0,1,2:T(2,128)(2,1)}), bf16[2,8,128,512]{3,0,1,2:T(2,128)(2,1)}, u32[]{:S(2)}, u32[]{:S(2)}) async-start(bf16[2,8,128,512]{3,0,1,2:T(2,128)(2,1)} %copy.88), calls=%async_computation.1 | async-start | bytes 4194304 | tf_op jit(solution)/shard_map/all_to_all | solution.py:22
  70.2 183.0 %all-gather.6.cloned.1.call-start = ((), (), s32[]{:S(2)}) async-start(), calls=%async_computation.11 | async-start | bytes 4456448 | tf_op jit(solution)/shard_map/all_gather | solution.py:33
  71.0 195.5 %all-gather.4.cloned.1.call-start = ((), (), s32[]{:S(2)}) async-start(), calls=%async_computation.10 | async-start | bytes 6291456 | tf_op jit(solution)/shard_map/all_gather | solution.py:43
  143.9 2.9 copy-start.1
  144.0 2.9 copy-start.11
  144.0 2.9 copy-start.13
  145.5 1.3 copy-start.4
  207.0 1.3 copy-start.2
  207.1 2.9 copy-start.10
  209.9 133.5 %all-gather.8.cloned.1.call-start = ((), (), s32[]{:S(2)}) async-start(), calls=%async_computation.12 | async-start | bytes 6291456 | tf_op jit(solution)/shard_map/all_gather | solution.py:55
  210.0 1.6 collective-permute-start
  211.7 13.5 %collective-permute-start.1 = (bf16[2048,128]{0,1:T(8,128)(2,1)S(1)}, bf16[2048,128]{0,1:T(8,128)(2,1)S(1)}, u32[]{:S(2)}, u32[]{:S(2)}) collective-permute-start(bf16[2048,128]{0,1:T(8,128)(2,1)S(1)} %maximum_select_fusion.5), channel_id=1, source_target_pairs={{0,4},{2,6},{4,0},{6,2},{8,12},{10,14},{12,8},{14,10},{16,20},{18,... | collective-permute-start | bytes 1572872 | tf_op jit(solution)/shard_map/ppermute | solution.py:37
  225.4 23.9 %collective-permute-start.2 = (bf16[2048,256]{0,1:T(8,128)(2,1)S(1)}, bf16[2048,256]{0,1:T(8,128)(2,1)}, u32[]{:S(2)}, u32[]{:S(2)}) collective-permute-start(bf16[2048,256]{0,1:T(8,128)(2,1)S(1)} %maximum_select_fusion.2), channel_id=1, source_target_pairs={{0,8},{2,10},{4,12},{6,14},{8,0},{10,2},{12,4},{14,6},{16,24},{18,... | collective-permute-start | bytes 3145736 | tf_op jit(solution)/shard_map/ppermute | solution.py:37
  225.8 561.8 %reduce-scatter.3.cloned.1.call-start = ((), (), s32[]{:S(2)}) async-start(), calls=%async_computation.13 | async-start | bytes 8912896 | tf_op jit(solution)/shard_map/reduce_scatter | solution.py:70
  251.8 91.6 %copy-start.7 = (bf16[2048,512]{0,1:T(8,128)(2,1)}, bf16[2048,512]{0,1:T(8,128)(2,1)S(1)}, u32[]{:S(2)}) copy-start(bf16[2048,512]{0,1:T(8,128)(2,1)S(1)} %maximum_select_fusion.1) | copy-start | bytes 6291460
  251.9 91.6 %collective-permute-start.3 = (bf16[2048,512]{0,1:T(8,128)(2,1)S(1)}, bf16[2048,512]{0,1:T(8,128)(2,1)}, u32[]{:S(2)}, u32[]{:S(2)}) collective-permute-start(bf16[2048,512]{0,1:T(8,128)(2,1)S(1)} %maximum_select_fusion.1), channel_id=1, source_target_pairs={{0,16},{2,18},{4,20},{6,22},{8,24},{10,26},{12,28},{14,30},{16,0},... | collective-permute-start | bytes 6291464 | tf_op jit(solution)/shard_map/ppermute | solution.py:37
  494.8 5.5 copy-start.6
  505.7 55.8 %all-to-all-start.5 = ((bf16[2,8,128,512]{3,1,0,2:T(8,128)(2,1)}), bf16[2,8,128,512]{3,1,0,2:T(8,128)(2,1)S(1)}, u32[]{:S(2)}, u32[]{:S(2)}) async-start(bf16[2,8,128,512]{3,1,0,2:T(8,128)(2,1)} %copy.99), calls=%async_computation.5 | async-start | bytes 4194304 | tf_op jit(solution)/shard_map/all_to_all | solution.py:81
  561.6 99.3 %all-to-all-start.3 = ((f32[2048,2,512]{0,2,1:T(8,128)}), f32[2048,2,512]{0,2,1:T(8,128)}, u32[]{:S(2)}, u32[]{:S(2)}) async-start(f32[2048,2,512]{0,2,1:T(8,128)} %bitcast.99), calls=%async_computation.3 | async-start | bytes 16777216 | tf_op jit(solution)/shard_map/all_to_all | solution.py:47
  568.6 221.0 %reduce-scatter.5.cloned.1.call-start = ((), (), s32[]{:S(2)}) async-start(), calls=%async_computation.14 | async-start | bytes 8912896 | tf_op jit(solution)/shard_map/reduce_scatter | solution.py:64
  587.1 5.5 copy-start.5
  587.1 5.5 copy-start.12
  587.1 5.5 copy-start.14
  660.8 70.0 %all-to-all-start.7 = ((bf16[2,128,8,512]{3,0,2,1:T(2,128)(2,1)}), bf16[2,128,8,512]{3,0,2,1:T(2,128)(2,1)}, u32[]{:S(2)}, u32[]{:S(2)}) async-start(bf16[2,128,8,512]{3,0,2,1:T(2,128)(2,1)} %copy.108), calls=%async_computation.7 | async-start | bytes 4194304 | tf_op jit(solution)/shard_map/all_to_all | solution.py:88
  673.1 63.1 %copy-start.3 = (bf16[2,128,8,512]{3,2,1,0:T(8,128)(2,1)S(1)}, bf16[2,128,8,512]{3,2,1,0:T(8,128)(2,1)}, u32[]{:S(2)}) copy-start(bf16[2,128,8,512]{3,2,1,0:T(8,128)(2,1)} %copy-done.2) | copy-start | bytes 6291460
  730.8 52.6 %all-to-all-start.6 = ((bf16[2,128,8,512]{3,0,2,1:T(2,128)(2,1)}), bf16[2,128,8,512]{3,0,2,1:T(2,128)(2,1)}, u32[]{:S(2)}, u32[]{:S(2)}) async-start(bf16[2,128,8,512]{3,0,2,1:T(2,128)(2,1)} %copy.103), calls=%async_computation.6 | async-start | bytes 4194304 | tf_op jit(solution)/shard_map/all_to_all | solution.py:94
  756.2 29.2 %copy-start.9 = (bf16[8,128,128]{2,1,0:T(8,128)(2,1)S(1)}, bf16[8,128,128]{2,1,0:T(8,128)(2,1)}, u32[]{:S(2)}) copy-start(bf16[8,128,128]{2,1,0:T(8,128)(2,1)} %param.9) | copy-start | bytes 786436
Sparse Core Ops, SparseCore 0:
  73.2 71.5 all-gather.5
  210.0 56.3 all-gather.3
  268.0 56.7 all-gather.7
  379.6 106.5 reduce-scatter.2
  583.3 132.8 reduce-scatter.4
